TPU v7x, 128 devices: a whole 4x4x4 slice. The times are simulated.
128 devices in a mesh: depth: 16 (over x_hi, y, core), seq: 8 (over z, x_lo).
Axes of the slice: x: 4 (x_hi: 2, x_lo: 2; x = x_hi * 2 + x_lo), y: 4, z: 4, core: 2. Of those that a mesh axis runs over, the one named last changes fastest.
Arguments:
- interfaces: bfloat16 [16, 1, 2048, 1024], P('depth', None, 'seq'), may hold values from -6 to 6
- doc_ids: int32 [1, 2048], replicated, may hold values from 0 to 3, never falling along the last dimension, each value on 1 to 1024 neighbouring positions
- w_attn: bfloat16 [16, 1, 4, 1024, 1024], P('depth'), may hold values from -0.1875 to 0.1875
- w_up: bfloat16 [16, 1, 1024, 4096], P('depth'), may hold values from -0.1875 to 0.1875
- w_down: bfloat16 [16, 1, 4096, 1024], P('depth'), may hold values from -0.09375 to 0.09375
- norm_gains: float32 [16, 1, 2, 1024], P('depth'), may hold values from 0.25 to 1.75
- coarse_gain: float32 [16, 1024], P('depth'), may hold values from 0 to 1
Outputs:
- relaxed: bfloat16 [16, 1, 2048, 1024], P('depth', None, 'seq')
Inputs may be any that keep to these rules, and one draw needn't show every extreme that they name: doc_ids never fall along a sequence and number the documents packed into it.
All inputs are finite; a program needn't handle non-finite values.
Results may differ from a plain program's by a relative error of at most 0.025.
Values may be sent and summed in bfloat16 or wider, within the bound.
A program may use at most 192 MiB of HBM per device.

v0:
```python
import jax
import jax.numpy as jnp
from jax import lax
from jax.sharding import Mesh
from jax.sharding import PartitionSpec as P

HEADS = 16
SEQ = ("seq_0", "seq_1")
DEPTH = ("depth_0", "depth_1", "depth_2")


def whole_of(x, axes, dim):
    for axis in reversed(axes):
        x = lax.all_gather(x, axis, axis=dim, tiled=True)
    return x


def passed_along(value, axis, steps):
    count = lax.axis_size(axis)
    first, last = (max(0, -steps), min(count, count - steps))
    return lax.ppermute(value, axis, [(source, source + steps) for source in range(first, last)])


def nothing_yet(x, identity):
    return jax.tree.map(
        lambda part, zero: jnp.zeros_like(part) + jnp.asarray(zero, part.dtype), x, identity
    )


def carried_in(x, axes, combine, identity):
    before = start = nothing_yet(x, identity)
    subtotal = x
    for axis in reversed(axes):
        length, mine = (lax.axis_size(axis), lax.axis_index(axis))
        pieces = jax.tree.map(
            lambda part, kind: lax.all_gather(part.astype(kind), axis),
            subtotal,
            (jnp.bfloat16, jnp.bfloat16),
        )
        inside, subtotal = (start, start)
        for k in range(length):
            passed = k < mine
            subtotal = combine(
                subtotal, jax.tree.map(lambda part, own: part[k].astype(own.dtype), pieces, x)
            )
            inside = jax.tree.map(lambda new, old: jnp.where(passed, new, old), subtotal, inside)
        before = combine(inside, before)
    return before


def rms_norm(value_tensor, gain):
    return (
        value_tensor
        * lax.rsqrt(jnp.mean(value_tensor * value_tensor, axis=-1, keepdims=True) + 1e-05)
        * gain
    )


def one_layer(states, attn_w, up_w, lowering_matrix, gain_pair, doc_ids):
    batch, rows, width = states.shape
    head_dim = width // HEADS
    score_scale = head_dim ** (-0.5)
    normed = rms_norm(states.astype(jnp.float32), gain_pair[0]).astype(jnp.bfloat16)
    flat = normed.reshape(-1, width)
    queries = (
        jnp.dot(flat, attn_w[0], preferred_element_type=jnp.float32)
        .astype(jnp.bfloat16)
        .reshape(batch, rows, HEADS, head_dim)
    )
    my_seq = lax.axis_index(SEQ)
    query_pos = my_seq * rows + jnp.arange(rows, dtype=jnp.int32)
    query_doc = lax.dynamic_slice_in_dim(doc_ids, my_seq * rows, rows, 1)
    pieces = whole_of(normed, SEQ, 1)
    count_rows = pieces.shape[1]
    flat_piece = pieces.reshape(-1, width)
    key_rows = (
        jnp.dot(flat_piece, attn_w[1], preferred_element_type=jnp.float32)
        .astype(jnp.bfloat16)
        .reshape(batch, count_rows, width)
    )
    value_rows = (
        jnp.dot(flat_piece, attn_w[2], preferred_element_type=jnp.float32)
        .astype(jnp.bfloat16)
        .reshape(batch, count_rows, width)
    )
    width_keys = key_rows.shape[1]
    lookup_vectors_per_head = key_rows.reshape(batch, width_keys, HEADS, head_dim)
    value_heads = value_rows.reshape(batch, width_keys, HEADS, head_dim)
    scores = (
        jnp.einsum(
            "sqhd,skhd->shqk", queries, lookup_vectors_per_head, preferred_element_type=jnp.float32
        )
        * score_scale
    )
    key_pos = jnp.arange(width_keys, dtype=jnp.int32)
    allowed = (key_pos[None, :] <= query_pos[:, None])[None] & (
        query_doc[:, :, None] == doc_ids[:, None, :]
    )
    weights = jnp.where(allowed[:, None], jnp.exp(scores), jnp.zeros_like(scores))
    numerator = jnp.einsum(
        "shqk,skhd->shqd",
        weights.astype(jnp.bfloat16),
        value_heads,
        preferred_element_type=jnp.float32,
    )
    numerator, denominator = (numerator, jnp.sum(weights, axis=-1))
    attended = (
        (numerator / denominator[..., None])
        .transpose(0, 2, 1, 3)
        .reshape(batch * rows, width)
        .astype(jnp.bfloat16)
    )
    mixed = states.astype(jnp.float32) + jnp.dot(
        attended, attn_w[3], preferred_element_type=jnp.float32
    ).reshape(batch, rows, width)
    second = rms_norm(mixed, gain_pair[1]).astype(jnp.bfloat16).reshape(-1, width)
    expanded = jax.nn.gelu(jnp.dot(second, up_w, preferred_element_type=jnp.float32)).astype(
        jnp.bfloat16
    )
    result = mixed + jnp.dot(expanded, lowering_matrix, preferred_element_type=jnp.float32).reshape(
        batch, rows, width
    )
    return result.astype(jnp.bfloat16)


def run_section(states, doc_ids, w_attn, w_up, w_down, norm_gains):
    states = one_layer(states, w_attn[0, 0], w_up[0, 0], w_down[0, 0], norm_gains[0, 0], doc_ids)
    return states


def on_device(interfaces, doc_ids, w_attn, w_up, w_down, norm_gains, coarse_gain):
    following = passed_along(interfaces, DEPTH, -1)
    fine = run_section(interfaces[0], doc_ids, w_attn, w_up, w_down, norm_gains)
    mismatch = fine[None].astype(jnp.float32) - following.astype(jnp.float32)

    def compose(earlier, later):
        return (later[0] * earlier[0], later[0][:, None, None, :] * earlier[1] + later[1])

    identity_map = (jnp.ones_like(coarse_gain), jnp.zeros_like(mismatch))
    prefix = carried_in((coarse_gain, mismatch), DEPTH, compose, identity_map)
    correction = prefix[1]
    corrected = (interfaces.astype(jnp.float32) + correction).astype(jnp.bfloat16)
    relaxed = run_section(corrected[0], doc_ids, w_attn, w_up, w_down, norm_gains)
    return relaxed[None]


def solution(mesh):
    split = Mesh(
        mesh.devices.reshape(2, 4, 2, 4, 2), ("depth_0", "depth_1", "depth_2", "seq_0", "seq_1")
    )
    in_specs = (
        P(DEPTH, None, SEQ, None),
        P(),
        P(DEPTH, None, None, None, None),
        P(DEPTH, None, None, None),
        P(DEPTH, None, None, None),
        P(DEPTH, None, None, None),
        P(DEPTH, None),
    )
    out_specs = P(DEPTH, None, SEQ, None)
    return jax.shard_map(
        on_device, mesh=split, in_specs=in_specs, out_specs=out_specs, check_vma=False
    )
```

profile of v0, /device:TPU:1, one launch (start us, length us, event | category | flops | bytes accessed | tf_op | source)
XLA Modules:
  0.0 368.9 jit_solution(1694150874440018408)
XLA Ops:
  6.5 0.8 fusion.201
  7.3 1.2 fusion.148
  8.6 2.0 fusion.150
  10.6 0.0 all-gather.11.cloned.1.call-update
  10.6 0.0 all-gather.13.cloned.1.call-start
  10.7 26.9 %all-gather.11.cloned.1.call-done = bf16[1,512,1024]{2,1,0:T(8,128)(2,1)} async-done(((bf16[1,256,1024]{2,1,0:T(8,128)(2,1)}), bf16[1,512,1024]{2,1,0:T(8,128)(2,1)}) %all-gather.11.cloned.1.call-update) | async-done | bytes 1048592 | tf_op jit(solution)/shard_map/all_gather | solution.py:14
  37.6 0.0 all-gather.13.cloned.1.call-update
  37.6 0.0 all-gather.23.cloned.1.call-start
  37.7 2.8 collective-permute-start
  40.4 2.5 fusion.105
  43.0 0.2 copy.12
  43.2 0.5 fusion.74
  43.8 44.9 %all-gather.13.cloned.1.call-done = bf16[1,2048,1024]{2,1,0:T(8,128)(2,1)} async-done(((bf16[1,512,1024]{2,1,0:T(8,128)(2,1)}), bf16[1,2048,1024]{2,1,0:T(8,128)(2,1)}) %all-gather.13.cloned.1.call-update) | async-done | bytes 4194320 | tf_op jit(solution)/shard_map/all_gather | solution.py:14
  88.7 7.4 %fusion.50 = bf16[2048,1024]{0,1:T(8,128)(2,1)S(1)} fusion(bf16[1,2048,1024]{2,1,0:T(8,128)(2,1)} %all-gather.13.cloned.1.call-done, bf16[1,1,4,1024,1024]{4,3,2,1,0:T(8,128)(2,1)} %param.9), kind=kOutput, calls=%fused_computation.44 | convolution fusion | flops 4297064448 | bytes 10485760 | tf_op jit(solution)/shard_map/dot_general | solution.py:77
  96.1 15.0 %fusion = (f32[16,256]{1,0:T(8,128)S(1)}, f32[16,256,2048]{2,1,0:T(8,128)}) fusion(pred[256,2048]{1,0:T(8,128)(4,1)S(1)} %fusion.74, bf16[256,16,64]{0,2,1:T(8,128)(2,1)S(1)} %bitcast.267, bf16[2048,16,64]{0,2,1:T(8,128)(2,1)S(1)} %bitcast.295), kind=kOutput, calls=%fused_computation.2 | convolution fusion | flops 1098903552 | bytes 38813696 | tf_op jit(solution)/shard_map/sqhd,skhd->shqk/dot_general | solution.py:90
  111.2 7.9 %fusion.53 = bf16[2048,1024]{0,1:T(8,128)(2,1)} fusion(bf16[1,2048,1024]{2,1,0:T(8,128)(2,1)S(1)} %copy-done.6, bf16[1,1,4,1024,1024]{4,3,2,1,0:T(8,128)(2,1)} %param.9), kind=kOutput, calls=%fused_computation.45 | convolution fusion | flops 4297064448 | bytes 10485760 | tf_op jit(solution)/shard_map/dot_general | solution.py:82
  119.1 15.1 %divide_convert_fusion.1 = bf16[16,256,64]{1,2,0:T(8,128)(2,1)S(1)} fusion(bf16[2048,16,64]{0,2,1:T(8,128)(2,1)} %bitcast.294, f32[16,256,2048]{2,1,0:T(8,128)} %get-tuple-element.20, pred[256,2048]{1,0:T(8,128)(4,1)S(1)} %fusion.74, f32[16,256]{1,0:T(8,128)S(1)} %get-tuple-element.19), kind=kOutput, calls=%fused_computation.150 | convolution fusion | flops 1099431936 | bytes 38813696 | tf_op jit(solution)/shard_map/shqk,skhd->shqd/dot_general | solution.py:100
  134.2 2.4 multiply_reduce_fusion.1
  136.7 11.5 %subtract_convert_fusion = bf16[1,1,256,1024]{3,2,1,0:T(8,128)(2,1)} fusion(bf16[1,1,256,1024]{3,2,1,0:T(8,128)(2,1)S(1)} %collective-permute-done, f32[256,1024]{1,0:T(8,128)S(1)} %get-tuple-element.22, bf16[1,1,4096,1024]{3,2,1,0:T(8,128)(2,1)} %param.11, bf16[1,1,1024,4096]{3,2,1,0:T(8,128)(2,1)} %param.10, f32[1024]{0:T(1024)S(1)} %bitcast.291, ...), kind=kOutput, calls=%fused_computation.147 | convolution fusion | flops 4306763776 | bytes 18879488 | tf_op jit(solution)/shard_map/dot_general | solution.py:120
  148.2 0.0 all-gather.23.cloned.1.call-update
  148.2 0.0 all-gather.15.cloned.1.call-start
  148.3 2.3 all-gather.2
  150.6 9.5 %all_gather.42 = bf16[4,1,1024]{2,1,0:T(2,128)(2,1)S(1)} all-gather(bf16[1,1,1024]{2,1,0:T(2,128)(2,1)S(1)} %multiply_convert_fusion.8), channel_id=1, replica_groups=mesh['depth_0'=2,'depth_1'=4,'depth_2'=2,'seq_0'=4,'seq_1'=2] {'depth_1'}, dimensions={0}, use_global_device_ids=true | all-gather | bytes 10240 | tf_op jit(solution)/shard_map/all_gather | solution.py:36
  160.1 0.7 all-gather.23.cloned.1.call-done
  160.9 2.2 fusion.147
  163.1 0.0 all-gather.15.cloned.1.call-update
  163.1 0.0 all-gather.17.cloned.1.call-start
  163.1 32.2 %all-gather.15.cloned.1.call-done = bf16[4,1,1,256,1024]{4,3,2,1,0:T(8,128)(2,1)} async-done(((bf16[1,1,1,256,1024]{4,3,2,1,0:T(8,128)(2,1)}), bf16[4,1,1,256,1024]{4,3,2,1,0:T(8,128)(2,1)}) %all-gather.15.cloned.1.call-update) | async-done | bytes 2097168 | tf_op jit(solution)/shard_map/all_gather | solution.py:36
  195.3 2.9 fusion.142
  198.2 0.0 all-gather.17.cloned.1.call-update
  198.2 0.0 all-gather.19.cloned.1.call-start
  198.3 4.7 %all_gather.43 = bf16[2,1,1024]{2,1,0:T(2,128)(2,1)S(1)} all-gather(bf16[1,1,1024]{2,1,0:T(2,128)(2,1)S(1)} %multiply_convert_fusion.9), channel_id=1, replica_groups=mesh['depth_0'=2,'depth_1'=4,'depth_2'=2,'seq_0'=4,'seq_1'=2] {'depth_0'}, dimensions={0}, use_global_device_ids=true | all-gather | bytes 6144 | tf_op jit(solution)/shard_map/all_gather | solution.py:36
  203.0 20.7 %all-gather.17.cloned.1.call-done = bf16[2,1,1,256,1024]{4,3,2,1,0:T(8,128)(2,1)} async-done(((bf16[1,1,1,256,1024]{4,3,2,1,0:T(8,128)(2,1)}), bf16[2,1,1,256,1024]{4,3,2,1,0:T(8,128)(2,1)}) %all-gather.17.cloned.1.call-update) | async-done | bytes 1048592 | tf_op jit(solution)/shard_map/all_gather | solution.py:36
  223.7 3.0 fusion.151
  226.6 1.0 fusion.153
  227.6 0.0 all-gather.19.cloned.1.call-update
  227.7 0.0 all-gather.21.cloned.1.call-start
  227.7 23.3 %all-gather.19.cloned.1.call-done = bf16[1,512,1024]{2,1,0:T(8,128)(2,1)} async-done(((bf16[1,256,1024]{2,1,0:T(8,128)(2,1)}), bf16[1,512,1024]{2,1,0:T(8,128)(2,1)}) %all-gather.19.cloned.1.call-update) | async-done | bytes 1048592 | tf_op jit(solution)/shard_map/all_gather | solution.py:14
  251.1 0.0 all-gather.21.cloned.1.call-update
  251.1 2.4 fusion.108
  253.4 0.2 copy.13
  253.7 48.5 %all-gather.21.cloned.1.call-done = bf16[1,2048,1024]{2,1,0:T(8,128)(2,1)} async-done(((bf16[1,512,1024]{2,1,0:T(8,128)(2,1)}), bf16[1,2048,1024]{2,1,0:T(8,128)(2,1)}) %all-gather.21.cloned.1.call-update) | async-done | bytes 4194320 | tf_op jit(solution)/shard_map/all_gather | solution.py:14
  302.1 7.4 %fusion.56 = bf16[2048,1024]{0,1:T(8,128)(2,1)S(1)} fusion(bf16[1,2048,1024]{2,1,0:T(8,128)(2,1)} %all-gather.21.cloned.1.call-done, bf16[1,1,4,1024,1024]{4,3,2,1,0:T(8,128)(2,1)} %param.9), kind=kOutput, calls=%fused_computation.46 | convolution fusion | flops 4297064448 | bytes 10485760 | tf_op jit(solution)/shard_map/dot_general | solution.py:77
  309.6 15.1 %fusion.2 = (f32[16,256]{1,0:T(8,128)S(1)}, f32[16,256,2048]{2,1,0:T(8,128)}) fusion(pred[256,2048]{1,0:T(8,128)(4,1)S(1)} %copy-done.3, bf16[256,16,64]{0,2,1:T(8,128)(2,1)S(1)} %bitcast.268, bf16[2048,16,64]{0,2,1:T(8,128)(2,1)S(1)} %bitcast.296), kind=kOutput, calls=%fused_computation.4 | convolution fusion | flops 1098903552 | bytes 38813696 | tf_op jit(solution)/shard_map/sqhd,skhd->shqk/dot_general | solution.py:90
  324.7 7.9 %fusion.59 = bf16[2048,1024]{0,1:T(8,128)(2,1)} fusion(bf16[1,2048,1024]{2,1,0:T(8,128)(2,1)S(1)} %copy-done.7, bf16[1,1,4,1024,1024]{4,3,2,1,0:T(8,128)(2,1)} %param.9), kind=kOutput, calls=%fused_computation.47 | convolution fusion | flops 4297064448 | bytes 10485760 | tf_op jit(solution)/shard_map/dot_general | solution.py:82
  332.6 15.3 %divide_convert_fusion = bf16[16,256,64]{1,2,0:T(8,128)(2,1)S(1)} fusion(bf16[2048,16,64]{0,2,1:T(8,128)(2,1)} %bitcast.293, f32[16,256,2048]{2,1,0:T(8,128)} %get-tuple-element.24, pred[256,2048]{1,0:T(8,128)(4,1)S(1)} %copy-done.3, f32[16,256]{1,0:T(8,128)S(1)} %get-tuple-element.23), kind=kOutput, calls=%fused_computation.146 | convolution fusion | flops 1099431936 | bytes 38813696 | tf_op jit(solution)/shard_map/shqk,skhd->shqd/dot_general | solution.py:100
  348.0 2.4 multiply_reduce_fusion
  350.4 11.5 %fusion.119 = bf16[1,1,256,1024]{3,2,1,0:T(8,128)(2,1)} fusion(f32[256,1024]{1,0:T(8,128)S(1)} %get-tuple-element.26, bf16[1,1,4096,1024]{3,2,1,0:T(8,128)(2,1)} %param.11, bf16[1,1,1024,4096]{3,2,1,0:T(8,128)(2,1)} %param.10, f32[256]{0:T(256)S(1)} %add_rsqrt_fusion, f32[1024]{0:T(1024)S(1)} %bitcast.292), kind=kOutput, calls=%fused_computation.105 | convolution fusion | flops 4305715200 | bytes 18355200 | tf_op jit(solution)/shard_map/dot_general | solution.py:120
  (32 shorter events, 0.2 us)
Async XLA Ops:
  6.5 31.1 %all-gather.11.cloned.1.call-start = ((), (), s32[]{:S(2)}) async-start(), calls=%async_computation | async-start | bytes 1572864 | tf_op jit(solution)/shard_map/all_gather | solution.py:14
  8.6 34.7 %copy-start.4 = (s32[1,2048]{1,0:T(1,128)S(1)}, s32[1,2048]{1,0:T(1,128)}, u32[]{:S(2)}) copy-start(s32[1,2048]{1,0:T(1,128)} %param.8) | copy-start | bytes 24580
  10.6 78.1 %all-gather.13.cloned.1.call-start = ((), (), s32[]{:S(2)}) async-start(), calls=%async_computation.1 | async-start | bytes 5242880 | tf_op jit(solution)/shard_map/all_gather | solution.py:14
  37.6 123.2 %all-gather.23.cloned.1.call-start = ((), (), s32[]{:S(2)}) async-start(), calls=%async_computation.6 | async-start | bytes 1572864 | tf_op jit(solution)/shard_map/all_gather | solution.py:36
  37.7 99.0 %collective-permute-start = (bf16[1,1,256,1024]{3,2,1,0:T(8,128)(2,1)}, bf16[1,1,256,1024]{3,2,1,0:T(8,128)(2,1)S(1)}, u32[]{:S(2)}, u32[]{:S(2)}) collective-permute-start(bf16[1,1,256,1024]{3,2,1,0:T(8,128)(2,1)} %param.7), channel_id=1, source_target_pairs={{8,0},{16,8},{24,16},{32,24},{40,32},{48,40},{56,48},{64,56},{72,6... | collective-permute-start | bytes 1572872 | tf_op jit(solution)/shard_map/ppermute | solution.py:21
  43.8 75.3 %copy-start.2 = (pred[256,2048]{1,0:T(8,128)(4,1)}, pred[256,2048]{1,0:T(8,128)(4,1)S(1)}, u32[]{:S(2)}) copy-start(pred[256,2048]{1,0:T(8,128)(4,1)S(1)} %fusion.74) | copy-start | bytes 1572868
  96.1 15.1 %copy-start.6 = (bf16[1,2048,1024]{2,1,0:T(8,128)(2,1)S(1)}, bf16[1,2048,1024]{2,1,0:T(8,128)(2,1)}, u32[]{:S(2)}) copy-start(bf16[1,2048,1024]{2,1,0:T(8,128)(2,1)} %all-gather.13.cloned.1.call-done) | copy-start | bytes 12582916
  119.1 15.2 %copy-start.1 = (bf16[1,1,256,1024]{3,2,1,0:T(8,128)(2,1)S(1)}, bf16[1,1,256,1024]{3,2,1,0:T(8,128)(2,1)}, u32[]{:S(2)}) copy-start(bf16[1,1,256,1024]{3,2,1,0:T(8,128)(2,1)} %param.7) | copy-start | bytes 1572868
  136.7 11.6 %copy-start.5 = (f32[1,1024]{1,0:T(1,128)S(1)}, f32[1,1024]{1,0:T(1,128)}, u32[]{:S(2)}) copy-start(f32[1,1024]{1,0:T(1,128)} %param.13) | copy-start | bytes 12292
  148.2 47.1 %all-gather.15.cloned.1.call-start = ((), (), s32[]{:S(2)}) async-start(), calls=%async_computation.2 | async-start | bytes 2621440 | tf_op jit(solution)/shard_map/all_gather | solution.py:36
  163.1 60.6 %all-gather.17.cloned.1.call-start = ((), (), s32[]{:S(2)}) async-start(), calls=%async_computation.3 | async-start | bytes 1572864 | tf_op jit(solution)/shard_map/all_gather | solution.py:36
  195.3 28.4 %copy-start = (bf16[4,1,1,256,1024]{4,3,2,1,0:T(8,128)(2,1)S(1)}, bf16[4,1,1,256,1024]{4,3,2,1,0:T(8,128)(2,1)}, u32[]{:S(2)}) copy-start(bf16[4,1,1,256,1024]{4,3,2,1,0:T(8,128)(2,1)} %all-gather.15.cloned.1.call-done) | copy-start | bytes 6291460
  198.2 52.8 %all-gather.19.cloned.1.call-start = ((), (), s32[]{:S(2)}) async-start(), calls=%async_computation.4 | async-start | bytes 1572864 | tf_op jit(solution)/shard_map/all_gather | solution.py:14
  227.7 74.5 %all-gather.21.cloned.1.call-start = ((), (), s32[]{:S(2)}) async-start(), calls=%async_computation.5 | async-start | bytes 5242880 | tf_op jit(solution)/shard_map/all_gather | solution.py:14
  253.6 55.9 %copy-start.3 = (pred[256,2048]{1,0:T(8,128)(4,1)S(1)}, pred[256,2048]{1,0:T(8,128)(4,1)}, u32[]{:S(2)}) copy-start(pred[256,2048]{1,0:T(8,128)(4,1)} %copy-done.2) | copy-start | bytes 1572868
  309.6 15.1 %copy-start.7 = (bf16[1,2048,1024]{2,1,0:T(8,128)(2,1)S(1)}, bf16[1,2048,1024]{2,1,0:T(8,128)(2,1)}, u32[]{:S(2)}) copy-start(bf16[1,2048,1024]{2,1,0:T(8,128)(2,1)} %all-gather.21.cloned.1.call-done) | copy-start | bytes 12582916
Sparse Core Ops, SparseCore 0:
  10.7 26.8 all-gather.10
  39.3 49.3 all-gather.12
  148.3 12.4 all-gather.22
  163.2 32.0 all-gather.14
  198.3 25.2 all-gather.16
  227.8 23.2 all-gather.18
  252.7 49.3 all-gather.20
where the time goes:
time: 374 us; the launch traced here: 369 us
  waiting for transfers between devices  197 us (53%)
  matrix products  124 us (33%)
  blocking collectives  16.5 us (4%)
  between operations  13.9 us (4%)
  other arithmetic  13 us (3%)
    all_gather x4, waiting for transfers between devices, whole_of(): x = lax.all_gather(x, axis, axis=dim, tiled=True)  144 us
    all_gather x3, waiting for transfers between devices, carried_in(): lax.all_gather(part.astype(kind), axis)  53.5 us
    dot_general x2, matrix products, one_layer(): jnp.einsum('shqk,skhd->shqd', weights.astype(jnp.bfloat16), value_heads,...  30.5 us
    dot_general x2, matrix products, one_layer(): jnp.einsum('sqhd,skhd->shqk', queries, lookup_vectors_per_head, preferred...  30.2 us
    dot_general x2, matrix products, one_layer(): jnp.dot(expanded, lowering_matrix, preferred_element_type=jnp.float32)  23 us
    all_gather x3, blocking collectives, carried_in(): lax.all_gather(part.astype(kind), axis)  16.5 us
    dot_general x2, matrix products, one_layer(): jnp.dot(flat_piece, attn_w[2], preferred_element_type=jnp.float32)  15.8 us
    dot_general x2, matrix products, one_layer(): jnp.dot(flat_piece, attn_w[1], preferred_element_type=jnp.float32)  14.8 us
  transfers between devices with their start and end apart: 8, of which 7 were waited for; matrix products, arithmetic and copies ran while one was open for 15% of the time, Pallas kernels for 0%

commit v1 on v0

v1 whole, which is shorter than its diff:
```python
import functools

import jax
import jax.numpy as jnp
from jax import lax
from jax.experimental import pallas as pl
from jax.experimental.pallas import tpu as pltpu
from jax.sharding import Mesh
from jax.sharding import PartitionSpec as P

D = 1024
FF = 4096
ROWS = 256
LANES = 128
HEAD = 64
GROUPS = 8
SPAN = 5
SEQ = ("seq_0", "seq_1")
DEPTH = ("depth_0", "depth_1", "depth_2")
MESH = pl.DeviceIdType.MESH
SEQ_STEPS = [(a, b) for a in range(4) for b in range(2) if (a, b) != (0, 0)]
DEPTH_STEPS = [(a, b) for a in range(2) for b in range(4) if (a, b) != (0, 0)]
K, Q, V, A = 0, 1, 2, 3
NT = (((1,), (1,)), ((), ()))


def dot(a, b):
    return jnp.dot(a, b, preferred_element_type=jnp.float32)


def rms(value, gain):
    return value * lax.rsqrt(jnp.mean(value * value, axis=-1, keepdims=True) + 1e-05) * gain


def kernel(
    x_ref, doc_ref, gain_ref, coarse_ref, wa_hbm, wu_hbm, wd_hbm, o_ref,
    wa, wu, wd, xs, nb, stage, stage_v, kr, qr, vr, mask, prob, stage_a, ar, mixed, second, acc,
    gains, fine, half_in, comp, depth_a, depth_u, depth_r, given, corrected,
    w_sem, send_sem, recv_sem, dsend_sem, drecv_sem, csend_sem, crecv_sem,
):
    h, y, core = (lax.axis_index(a) for a in DEPTH)
    z, c = (lax.axis_index(a) for a in SEQ)
    me = 2 * z + c
    chip = 4 * h + y

    def seq_peer(step):
        pz, pc = lax.rem(z + step[0], 4), lax.rem(c + step[1], 2)
        return (h, y, core, pz, pc), 2 * pz + pc

    def seq_from(step):
        pz, pc = lax.rem(z + 4 - step[0], 4), lax.rem(c + step[1], 2)
        return 2 * pz + pc

    def depth_peer(step):
        ph, py = lax.rem(h + step[0], 2), lax.rem(y + step[1], 4)
        return (ph, py, core, z, c), 4 * ph + py

    partner = (h, y, 1 - core, z, c)

    def weight(i):
        if i < 4:
            return pltpu.make_async_copy(wa_hbm.at[i], wa.at[i], w_sem.at[i])
        if i == 4:
            return pltpu.make_async_copy(wu_hbm, wu, w_sem.at[4])
        return pltpu.make_async_copy(wd_hbm, wd, w_sem.at[5])

    for i in (1, 0, 2, 3, 4, 5):
        weight(i).start()

    barrier = pltpu.get_barrier_semaphore()
    for step in SEQ_STEPS:
        pl.semaphore_signal(barrier, inc=1, device_id=seq_peer(step)[0], device_id_type=MESH)
    for step in DEPTH_STEPS:
        pl.semaphore_signal(barrier, inc=1, device_id=depth_peer(step)[0], device_id_type=MESH)
    pl.semaphore_signal(barrier, inc=1, device_id=partner, device_id_type=MESH)
    pl.semaphore_wait(barrier, 15)

    xs[...] = x_ref[...]

    def remote(src, dst, ss, rs, dev):
        return pltpu.make_async_remote_copy(
            src_ref=src, dst_ref=dst, send_sem=ss, recv_sem=rs, device_id=dev, device_id_type=MESH
        )

    gain_swap = remote(coarse_ref, gains.at[8], csend_sem.at[0], crecv_sem.at[0], partner)
    gain_swap.start()

    def gain_copy(i, step):
        dev, _ = depth_peer(step)
        return remote(
            gains.at[9], gains.at[chip], dsend_sem.at[2, i], drecv_sem.at[2, chip], dev
        )

    def seq_copy(p, kind, i, step):
        dev, dest = seq_peer(step)
        src = (stage.at[0, dest], stage.at[1, dest], stage_v.at[dest], stage_a.at[dest])[kind]
        dst = (kr, qr, vr, ar)[kind].at[p, me]
        return remote(src, dst, send_sem.at[kind, i], recv_sem.at[p, kind, me], dev)

    def seq_arrival(p, kind, i, step):
        who = seq_from(step)
        dst = (kr, qr, vr, ar)[kind].at[p, who]
        dev, _ = seq_peer(step)
        return remote(dst, dst, send_sem.at[kind, i], recv_sem.at[p, kind, who], dev)

    def send_all(p, kind):
        for i, step in enumerate(SEQ_STEPS):
            seq_copy(p, kind, i, step).start()

    def wait_all(p, kind):
        for i, step in enumerate(SEQ_STEPS):
            seq_arrival(p, kind, i, step).wait_recv()

    def one_pass(p, carry):
        first = p == 0
        nb[...] = rms(xs[...].astype(jnp.float32), gain_ref[0:1]).astype(jnp.bfloat16)

        def project(which, store):
            @pl.when(first)
            def _():
                weight(which).wait()

            def tile(t, carry):
                cols = pl.ds(pl.multiple_of(t * 256, 256), 256)
                store(t, dot(nb[...], wa[which, :, cols]).astype(jnp.bfloat16))
                return carry

            lax.fori_loop(0, 4, tile, 0)

        def store_k(t, r):
            stage[0, 2 * t] = r[:, :LANES]
            stage[0, 2 * t + 1] = r[:, LANES:]

        def store_q(t, r):
            r = r * jnp.bfloat16(0.125)
            stage[1, 2 * t] = r[:, :LANES]
            stage[1, 2 * t + 1] = r[:, LANES:]

        def store_v(t, r):
            r = r.T
            stage_v[2 * t] = r[:LANES]
            stage_v[2 * t + 1] = r[LANES:]

        project(1, store_k)
        send_all(p, K)
        kr[p, me] = stage[0, me]
        project(0, store_q)
        send_all(p, Q)
        qr[p, me] = stage[1, me]
        project(2, store_v)
        send_all(p, V)
        vr[p, me] = stage_v[me]

        @pl.when(first)
        def _():
            gain_swap.wait()
            gains[9] = coarse_ref[...] * gains[8]
            gains[chip] = gains[9]
            for i, step in enumerate(DEPTH_STEPS):
                gain_copy(i, step).start()

            def build(qb, carry):
                doc_q = doc_ref[qb]

                def inner(d, carry):
                    kb = qb - d
                    doc_k = jnp.broadcast_to(doc_ref[kb], (LANES, ROWS)).T
                    doc_k = jnp.concatenate([doc_k, doc_k], axis=1)
                    kpos = lax.broadcasted_iota(jnp.int32, (ROWS, ROWS), 0) - d * ROWS
                    qpos = lax.broadcasted_iota(jnp.int32, (ROWS, ROWS), 1)
                    ok = (kpos <= qpos) & (doc_k == doc_q)
                    mask[qb * SPAN + d] = jnp.where(ok, jnp.inf, 0.0).astype(jnp.bfloat16)
                    return carry

                return lax.fori_loop(0, jnp.minimum(qb, SPAN - 1) + 1, inner, carry)

            lax.fori_loop(0, GROUPS, build, 0)

        wait_all(p, K)
        wait_all(p, Q)

        def scores(qb, count):
            q = qr[p, qb]
            lane = lax.broadcasted_iota(jnp.int32, (ROWS, LANES), 1)
            parts = [
                jnp.where(lane < HEAD, q, jnp.zeros_like(q)),
                jnp.where(lane < HEAD, jnp.zeros_like(q), q),
            ]
            for d in range(count):
                keys = kr[p, qb - d]
                m = mask[qb * SPAN + d]
                for i in range(2):
                    s = lax.dot_general(keys, parts[i], NT, preferred_element_type=jnp.float32)
                    e = jnp.exp(s).astype(jnp.bfloat16)
                    prob[i, qb * SPAN + d] = jnp.minimum(e, m)

        for qb in range(SPAN - 1):
            scores(qb, qb + 1)

        def late(qb, carry):
            scores(qb, SPAN)
            return carry

        lax.fori_loop(SPAN - 1, GROUPS, late, 0)

        wait_all(p, V)
        ones = jnp.ones((16, ROWS), jnp.bfloat16)

        def attend(qb):
            def inner(d, carry):
                vt = vr[p, qb - d]
                out = []
                for i in range(2):
                    lhs = jnp.concatenate([vt[i * HEAD:(i + 1) * HEAD], ones], axis=0)
                    out.append(carry[i] + dot(lhs, prob[i, qb * SPAN + d]))
                return tuple(out)

            start = jnp.zeros((HEAD + 16, ROWS), jnp.float32)
            nums = lax.fori_loop(0, jnp.minimum(qb, SPAN - 1) + 1, inner, (start, start))
            both = [n[:HEAD] / n[HEAD:HEAD + 1] for n in nums]
            return jnp.concatenate(both, axis=0).T.astype(jnp.bfloat16)

        for i, step in enumerate(SEQ_STEPS):
            _, dest = seq_peer(step)
            stage_a[dest] = attend(dest)
            seq_copy(p, A, i, step).start()
        ar[p, me] = attend(me)

        @pl.when(first)
        def _():
            weight(3).wait()

        wait_all(p, A)
        attended = jnp.concatenate([ar[p, j] for j in range(GROUPS)], axis=1)
        nb[...] = attended

        def project_out(t, carry):
            cols = pl.ds(pl.multiple_of(t * 256, 256), 256)
            mixed[:, cols] = xs[:, cols].astype(jnp.float32) + dot(nb[...], wa[3, :, cols])
            return carry

        lax.fori_loop(0, 4, project_out, 0)
        second[...] = rms(mixed[...], gain_ref[1:2]).astype(jnp.bfloat16)

        @pl.when(first)
        def _():
            weight(4).wait()
            weight(5).wait()

        def feed(t, carry):
            cols = pl.ds(pl.multiple_of(t * 512, 512), 512)
            hidden = jax.nn.gelu(dot(second[...], wu[:, cols])).astype(jnp.bfloat16)
            mixed[...] += dot(hidden, wd[cols, :])
            return carry

        lax.fori_loop(0, FF // 512, feed, 0)

        for kind in (K, Q, V, A):
            for i, step in enumerate(SEQ_STEPS):
                seq_copy(p, kind, i, step).wait_send()

        @pl.when(first)
        def _():
            exchange()

        return carry

    def depth_copy(stage_no, i, step):
        dev, dest = depth_peer(step)
        if stage_no == 0:
            src = comp.at[pl.ds(pl.multiple_of(dest * 16, 16), 16)]
            dst = depth_a.at[chip]
        else:
            src, dst = depth_u.at[dest], depth_r.at[chip]
        return remote(src, dst, dsend_sem.at[stage_no, i], drecv_sem.at[stage_no, chip], dev)

    def depth_arrival(stage_no, i, step):
        ph, py = lax.rem(h + step[0], 2), lax.rem(y + 4 - step[1], 4)
        who = 4 * ph + py
        dst = (depth_a, depth_r, gains)[stage_no].at[who]
        dev, _ = depth_peer(step)
        return remote(dst, dst, dsend_sem.at[stage_no, i], drecv_sem.at[stage_no, who], dev)

    def exchange():
        lead = jnp.where((h + y + core) == 0, 0.0, 1.0)
        gain = coarse_ref[...]
        a = mixed[...].astype(jnp.bfloat16).astype(jnp.float32)
        fine[...] = (a - (lead * gain) * x_ref[...].astype(jnp.float32)).astype(jnp.bfloat16)
        theirs = pl.ds(pl.multiple_of((1 - core) * 128, 128), 128)
        mine = pl.ds(pl.multiple_of(core * 128, 128), 128)
        swap = remote(fine.at[theirs], half_in, csend_sem.at[1], crecv_sem.at[1], partner)
        swap.start()
        swap.wait()
        is_low = core == 0
        own, other = fine[mine, :].astype(jnp.float32), half_in[...].astype(jnp.float32)
        low, high = jnp.where(is_low, own, other), jnp.where(is_low, other, own)
        gain_low = jnp.where(is_low, gain, gains[8])
        gain_high = jnp.where(is_low, gains[8], gain)
        comp[...] = (high + gain_high * low).astype(jnp.bfloat16)
        for i, step in enumerate(DEPTH_STEPS):
            depth_copy(0, i, step).start()
        depth_a[chip] = comp[pl.ds(pl.multiple_of(chip * 16, 16), 16), :]
        for i, step in enumerate(DEPTH_STEPS):
            gain_copy(i, step).wait_send()
            depth_arrival(2, i, step).wait_recv()
            depth_arrival(0, i, step).wait_recv()
        u = jnp.zeros((16, D), jnp.float32)
        for k in range(8):
            depth_u[k] = u.astype(jnp.bfloat16)
            u = depth_a[k].astype(jnp.float32) + gains[k] * u
        for i, step in enumerate(DEPTH_STEPS):
            depth_copy(1, i, step).start()
        depth_r[chip] = depth_u[chip]
        for i, step in enumerate(DEPTH_STEPS):
            depth_arrival(1, i, step).wait_recv()
            depth_copy(0, i, step).wait_send()
            depth_copy(1, i, step).wait_send()
        back = jnp.concatenate([depth_r[k] for k in range(8)], axis=0).astype(jnp.float32)
        own, other = fine[mine, :].astype(jnp.float32), half_in[...].astype(jnp.float32)
        low = jnp.where(is_low, own, other)
        after = low + gain_low * back
        given[...] = jnp.where(is_low, after, back).astype(jnp.bfloat16)
        give = remote(given, corrected.at[mine], csend_sem.at[2], crecv_sem.at[2], partner)
        give.start()
        keep = jnp.where(is_low, back, after).astype(jnp.bfloat16)
        xs[mine, :] = keep
        give.wait_send()
        remote(given, corrected.at[theirs], csend_sem.at[2], crecv_sem.at[2], partner).wait_recv()
        xs[theirs, :] = corrected[theirs, :]

        @pl.when((h + y + core) == 0)
        def _():
            xs[...] = x_ref[...]

    lax.fori_loop(0, 2, one_pass, 0)
    o_ref[...] = mixed[...].astype(jnp.bfloat16)


def on_device(interfaces, doc_ids, w_attn, w_up, w_down, norm_gains, coarse_gain):
    x = interfaces.reshape(ROWS, D)
    doc = doc_ids.astype(jnp.float32).reshape(GROUPS, 1, ROWS)
    bf, f32 = jnp.bfloat16, jnp.float32
    vmem = pl.BlockSpec(memory_space=pltpu.VMEM)
    hbm = pl.BlockSpec(memory_space=pl.ANY)
    out = pl.pallas_call(
        kernel,
        out_shape=jax.ShapeDtypeStruct((ROWS, D), bf),
        in_specs=[vmem] * 4 + [hbm] * 3,
        out_specs=vmem,
        scratch_shapes=[
            pltpu.VMEM((4, D, D), bf),
            pltpu.VMEM((D, FF), bf),
            pltpu.VMEM((FF, D), bf),
            pltpu.VMEM((ROWS, D), bf),
            pltpu.VMEM((ROWS, D), bf),
            pltpu.VMEM((2, GROUPS, ROWS, LANES), bf),
            pltpu.VMEM((GROUPS, LANES, ROWS), bf),
            pltpu.VMEM((2, GROUPS, ROWS, LANES), bf),
            pltpu.VMEM((2, GROUPS, ROWS, LANES), bf),
            pltpu.VMEM((2, GROUPS, LANES, ROWS), bf),
            pltpu.VMEM((GROUPS * SPAN, ROWS, ROWS), bf),
            pltpu.VMEM((2, GROUPS * SPAN, ROWS, ROWS), bf),
            pltpu.VMEM((GROUPS, ROWS, LANES), bf),
            pltpu.VMEM((2, GROUPS, ROWS, LANES), bf),
            pltpu.VMEM((ROWS, D), f32),
            pltpu.VMEM((ROWS, D), bf),
            pltpu.VMEM((8, 128), f32),
            pltpu.VMEM((10, 1, D), f32),
            pltpu.VMEM((ROWS, D), bf),
            pltpu.VMEM((128, D), bf),
            pltpu.VMEM((128, D), bf),
            pltpu.VMEM((8, 16, D), bf),
            pltpu.VMEM((8, 16, D), bf),
            pltpu.VMEM((8, 16, D), bf),
            pltpu.VMEM((128, D), bf),
            pltpu.VMEM((ROWS, D), bf),
            pltpu.SemaphoreType.DMA((6,)),
            pltpu.SemaphoreType.DMA((4, 7)),
            pltpu.SemaphoreType.DMA((2, 4, 8)),
            pltpu.SemaphoreType.DMA((3, 7)),
            pltpu.SemaphoreType.DMA((3, 8)),
            pltpu.SemaphoreType.DMA((3,)),
            pltpu.SemaphoreType.DMA((3,)),
        ],
        compiler_params=pltpu.CompilerParams(
            collective_id=0, has_side_effects=True, vmem_limit_bytes=60 * 2**20
        ),
        name="cycle",
    )(
        x,
        doc,
        norm_gains.reshape(2, D),
        coarse_gain.reshape(1, D),
        w_attn.reshape(4, D, D),
        w_up.reshape(D, FF),
        w_down.reshape(FF, D),
    )
    return out.reshape(1, 1, ROWS, D)


def solution(mesh):
    split = Mesh(
        mesh.devices.reshape(2, 4, 2, 4, 2), ("depth_0", "depth_1", "depth_2", "seq_0", "seq_1")
    )
    in_specs = (
        P(DEPTH, None, SEQ, None),
        P(),
        P(DEPTH, None, None, None, None),
        P(DEPTH, None, None, None),
        P(DEPTH, None, None, None),
        P(DEPTH, None, None, None),
        P(DEPTH, None),
    )
    out_specs = P(DEPTH, None, SEQ, None)
    return jax.shard_map(
        on_device, mesh=split, in_specs=in_specs, out_specs=out_specs, check_vma=False
    )
```

time: 374 us -> 112 us (0.30); the launches traced: 369 us -> 112 us
  waiting for transfers between devices: 197 us -> 0 us
  matrix products: 124 us -> 0 us
  Pallas kernels: 0 us -> 109 us
  blocking collectives: 16.5 us -> 0 us
  between operations: 13.9 us -> 0.01 us
  other arithmetic: 13 us -> 1.3 us
    all_gather x7 -> x0, waiting for transfers between devices: 197 us -> none  [the longest x4 144 us: whole_of(): x = lax.all_gather(x, axis, axis=dim, tiled=True)]
    dot_general x14 -> x0, matrix products: 124 us -> none  [the longest x2 30.5 us: one_layer(): jnp.einsum('shqk,skhd->shqd', weights.astype(jnp.bfloat16), value_heads,...]
    pallas_call x0 -> x1, Pallas kernels: none -> 109 us  [on_device(): pl.pallas_call(kernel, out_shape=jax.ShapeDtypeStruct((ROWS, D), bf), in_...]
    all_gather x3 -> x0, blocking collectives: 16.5 us -> none  [carried_in(): lax.all_gather(part.astype(kind), axis)]
    convert_element_type x9 -> x1, other arithmetic: 8.17 us -> 1.3 us  [on_device(): doc = doc_ids.astype(jnp.float32).reshape(GROUPS, 1, ROWS)]
    reduce_sum x2 -> x0, other arithmetic: 4.19 us -> none  [rms_norm(): jnp.mean(value_tensor * value_tensor, axis=-1, keepdims=True) + 1e-05]
  transfers between devices with their start and end apart: 8 -> 0, of which waited for: 7 -> 0; matrix products, arithmetic and copies ran while one was open for 15% -> 0% of each run, Pallas kernels for 0% -> 0%
where the time goes in v1:
time: 112 us
  Pallas kernels  109 us (97%)
  local copies, waits for them, and re-layouts  1.87 us (2%)
  other arithmetic  1.3 us (1%)
    pallas_call x1, Pallas kernels, on_device(): pl.pallas_call(kernel, out_shape=jax.ShapeDtypeStruct((ROWS, D), bf), in_...  109 us

profile of v1, /device:TPU:1, one launch (start us, length us, event | category | flops | bytes accessed | tf_op | source)
XLA Modules:
  0.0 112.0 jit_solution(10950392859295942224)
XLA Ops:
  0.0 1.3 %convert_element_type.3 = f32[1,2048]{1,0:T(1,128)} convert(s32[1,2048]{1,0:T(1,128)} %param.8) | non-fusion elementwise | flops 2048 | bytes 16384 | tf_op jit(solution)/shard_map/convert_element_type | solution.py:341
  1.3 108.8 %cycle.1 = bf16[256,1024]{1,0:T(8,128)(2,1)} custom-call(bf16[256,1024]{1,0:T(8,128)(2,1)} %bitcast.11, f32[8,1,256]{2,1,0:T(1,128)} %bitcast.12, f32[2,1024]{1,0:T(2,128)} %bitcast.13, f32[1,1024]{1,0:T(1,128)} %coarse_ref.1, bf16[4,1024,1024]{2,1,0:T(8,128)(2,1)} %bitcast.7, bf16[1024,4096]{1,0:T(8,128)(2,1)} %bitcast.8, bf16[4096,1024]{1,0:T(8,128)(2,1)} %bitcast.9), custom_call_target="tpu_custom_call" | custom-call | tf_op jit(solution)/shard_map/cycle/pallas_call | solution.py:345
  110.1 1.9 %copy.9 = bf16[1,1,256,1024]{3,2,1,0:T(8,128)(2,1)} copy(bf16[1,1,256,1024]{3,2,1,0:T(8,128)(2,1)} %bitcast.10) | data formatting | bytes 1048576

commit v2 on v0

v2 whole, which is shorter than its diff:
```python
import functools

import jax
import jax.numpy as jnp
from jax import lax
from jax.experimental import pallas as pl
from jax.experimental.pallas import tpu as pltpu
from jax.sharding import Mesh
from jax.sharding import PartitionSpec as P

D = 1024
FF = 4096
ROWS = 256
LANES = 128
HEAD = 64
GROUPS = 8
SPAN = 5
SEQ = ("seq_0", "seq_1")
DEPTH = ("depth_0", "depth_1", "depth_2")
MESH = pl.DeviceIdType.MESH
K, Q, V, A = 0, 1, 2, 4
NT = (((1,), (1,)), ((), ()))


def dot(a, b):
    return jnp.dot(a, b, preferred_element_type=jnp.float32)


def each(count, action):
    def body(i, carry):
        action(i)
        return carry

    lax.fori_loop(0, count, body, 0)


def row_step(u):
    return (2 - u) + lax.div(u, 2) * (7 - 2 * u)


def seq_step(i):
    u = lax.div(i, 2)
    return row_step(u), 1 - (i - 2 * u)


def depth_step(i):
    u = lax.div(i + 1, 4)
    return u, i + 1 - 4 * u


def gelu(x):
    inner = x * (x * x * (0.044715 * 0.7978845608028654) + 0.7978845608028654)
    part = 0.5 * x
    return part * jnp.tanh(inner) + part


def rms(value, gain):
    return value * lax.rsqrt(jnp.mean(value * value, axis=-1, keepdims=True) + 1e-05) * gain


def kernel(
    x_hbm, doc_hbm, gain_hbm, coarse_hbm, wa_hbm, wu_hbm, wd_hbm, o_ref,
    x_ref, doc_ref, gain_ref, coarse_ref, wa, wu, wd, xs, nb, stage, stage_v, kr, qr, vr, mask, prob, stage_a, ar, mixed, hidden,
    gains, fine, half_in, comp, depth_a, depth_u, depth_r, given, corrected,
    in_sem, w_sem, wide_sem, send_sem, recv_sem, g_sem, dsend_sem, drecv_sem, csend_sem, crecv_sem,
):
    h, y, core = (lax.axis_index(a) for a in DEPTH)
    z, c = (lax.axis_index(a) for a in SEQ)
    me = 2 * z + c
    chip = 4 * h + y
    partner = (h, y, 1 - core, z, c)

    def seq_peer(dz, dx):
        pz, pc = lax.rem(z + 4 + dz, 4), lax.rem(c + dx, 2)
        return (h, y, core, pz, pc), 2 * pz + pc

    def depth_peer(dh, dy):
        ph, py = lax.rem(h + dh, 2), lax.rem(y + 4 + dy, 4)
        return (ph, py, core, z, c), 4 * ph + py

    def remote(src, dst, ss, rs, dev):
        return pltpu.make_async_remote_copy(
            src_ref=src, dst_ref=dst, send_sem=ss, recv_sem=rs, device_id=dev, device_id_type=MESH
        )

    def tile_cols(n):
        return pl.ds(pl.multiple_of(lax.rem(z + row_step(n), 4) * 256, 256), 256)

    def narrow(which, n):
        cols = tile_cols(n)
        return pltpu.make_async_copy(
            wa_hbm.at[which, :, cols], wa.at[which, :, cols], w_sem.at[which, n]
        )

    def wide(i):
        src, dst = ((wu_hbm, wu), (wd_hbm, wd))[i]
        return pltpu.make_async_copy(src, dst, wide_sem.at[i])

    def wide_out(j):
        i = lax.rem(j, 2)
        rows = pl.ds(pl.multiple_of(j * HEAD, HEAD), HEAD)
        place = pl.ds(pl.multiple_of(i * 512 + lax.div(j, 2) * HEAD, HEAD), HEAD)
        return pltpu.make_async_copy(wa_hbm.at[3, rows], wa.at[3, place], wide_sem.at[2])

    def wide_out_total():
        return pltpu.make_async_copy(wa_hbm.at[3], wa.at[3], wide_sem.at[2])

    def entry(i):
        src = (x_hbm, gain_hbm, x_hbm, doc_hbm, coarse_hbm)[i]
        dst = (xs, gain_ref, x_ref, doc_ref, coarse_ref)[i]
        return pltpu.make_async_copy(src, dst, in_sem.at[i])

    entry(0).start()
    entry(1).start()
    each(4, lambda n: narrow(1, n).start())

    barrier = pltpu.get_barrier_semaphore()

    def greet(dev):
        pl.semaphore_signal(barrier, inc=1, device_id=dev, device_id_type=MESH)

    each(7, lambda i: greet(seq_peer(*seq_step(i))[0]))
    each(7, lambda i: greet(depth_peer(*depth_step(i))[0]))
    greet(partner)
    entry(0).wait()
    entry(1).wait()
    each(4, lambda n: narrow(0, n).start())
    each(4, lambda n: narrow(2, n).start())
    for i in range(2, 5):
        entry(i).start()

    gain_swap = remote(coarse_ref, gains.at[8], csend_sem.at[2, 0], crecv_sem.at[2, 0], partner)

    def gain_copy(i):
        dev, _ = depth_peer(*depth_step(i))
        return remote(gains.at[9], gains.at[chip], g_sem.at[0], g_sem.at[1], dev)

    def gain_total():
        some = gains.at[pl.ds(0, 7)]
        return remote(some, some, g_sem.at[0], g_sem.at[1], partner)

    def seq_copy(p, kind, i):
        dev, dest = seq_peer(*seq_step(i))
        if kind == K:
            src, dst = stage.at[0, dest], kr.at[p, me]
        elif kind == Q:
            src, dst = stage.at[1, dest], qr.at[p, me]
        else:
            src, dst = stage_v.at[kind - V, dest], vr.at[p, kind - V, me]
        return remote(src, dst, send_sem.at[kind], recv_sem.at[p, kind], dev)

    def back_copy(p, i, dest):
        pz = lax.div(dest, 2)
        dev = (h, y, core, pz, dest - 2 * pz)
        return remote(
            stage_a.at[i, dest], ar.at[p, i, me], send_sem.at[A + i], recv_sem.at[p, A + i], dev
        )

    def total(p, kind):
        seven = pl.ds(0, 7)
        if kind == K:
            some = kr.at[p, seven]
        elif kind == Q:
            some = qr.at[p, seven]
        elif kind < A:
            some = vr.at[p, kind - V, seven]
        else:
            some = ar.at[p, kind - A, seven]
        return remote(some, some, send_sem.at[kind], recv_sem.at[p, kind], partner)

    lane = lax.broadcasted_iota(jnp.int32, (ROWS, LANES), 1)

    def one_pass(p, carry):
        first = p == 0
        nb[...] = rms(xs[...].astype(jnp.float32), gain_ref[0:1]).astype(jnp.bfloat16)

        def project(which, kind, store):
            def tile(u):
                @pl.when(first)
                def _():
                    narrow(which, u).wait()

                base = 2 * lax.rem(z + row_step(u), 4)
                store(base, dot(nb[...], wa[which, :, tile_cols(u)]).astype(jnp.bfloat16))
                if kind == K:

                    @pl.when(first & (u == 0))
                    def _():
                        pl.semaphore_wait(barrier, 15)

                if kind != V:
                    seq_copy(p, kind, 2 * u).start()

                    @pl.when(u < 3)
                    def _():
                        seq_copy(p, kind, 2 * u + 1).start()

            each(4, tile)
            if kind == V:
                each(7, lambda i: seq_copy(p, V, i).start())
                each(7, lambda i: seq_copy(p, V + 1, i).start())

        def store_k(base, r):
            stage[0, base] = r[:, :LANES]
            stage[0, base + 1] = r[:, LANES:]

        def store_q(base, r):
            r = r * jnp.bfloat16(0.125)
            stage[1, base] = r[:, :LANES]
            stage[1, base + 1] = r[:, LANES:]

        def store_v(base, r):
            r = r.T
            for j in range(2):
                for i in range(2):
                    stage_v[i, base + j] = r[j * LANES + i * HEAD:j * LANES + (i + 1) * HEAD]

        project(1, K, store_k)
        kr[p, me] = stage[0, me]
        project(0, Q, store_q)
        qr[p, me] = stage[1, me]
        project(2, V, store_v)
        for i in range(2):
            vr[p, i, me] = stage_v[i, me]

        @pl.when(first)
        def _():
            each(16, lambda j: wide_out(j).start())
            wide(0).start()
            wide(1).start()
            for i in range(2, 5):
                entry(i).wait()
            gain_swap.start()
            gain_swap.wait()
            gains[9] = coarse_ref[...] * gains[8]
            gains[chip] = gains[9]
            each(7, lambda i: gain_copy(i).start())

            def build(qb, carry):
                doc_q = doc_ref[qb].astype(jnp.float32)

                def inner(d, carry):
                    doc_k = doc_ref[qb - d].astype(jnp.float32)
                    doc_k = jnp.broadcast_to(doc_k, (LANES, ROWS)).T
                    doc_k = jnp.concatenate([doc_k, doc_k], axis=1)
                    kpos = lax.broadcasted_iota(jnp.int32, (ROWS, ROWS), 0) - d * ROWS
                    qpos = lax.broadcasted_iota(jnp.int32, (ROWS, ROWS), 1)
                    ok = (kpos <= qpos) & (doc_k == doc_q)
                    mask[qb * SPAN + d] = jnp.where(ok, jnp.inf, 0.0).astype(jnp.bfloat16)
                    return carry

                return lax.fori_loop(0, jnp.minimum(qb, SPAN - 1) + 1, inner, carry)

            lax.fori_loop(0, GROUPS, build, 0)

        total(p, K).wait_recv()
        total(p, Q).wait_recv()
        own = jnp.where(me >= 4, me - 4, jnp.where((me == 0) | (me == 3), 4, 5))

        def unit_of(t):
            unit = lax.rem(own + 1 + t, 6)
            paired = unit >= 4
            low = jnp.where(paired, unit - 4, unit + 4)
            high = jnp.where(paired, 3 - low, low)
            split = jnp.where(paired, low + 1, SPAN)
            return paired, low, high, split

        def weigh(t):
            _, low, high, split = unit_of(t)
            for j in range(SPAN):
                is_low = j < split
                qb = jnp.where(is_low, low, high)
                d = jnp.where(is_low, j, j - split)
                q = qr[p, qb]
                zero = jnp.zeros_like(q)
                parts = jnp.where(lane < HEAD, q, zero), jnp.where(lane < HEAD, zero, q)
                keys = kr[p, qb - d]
                m = mask[qb * SPAN + d]
                for i in range(2):
                    s = lax.dot_general(keys, parts[i], NT, preferred_element_type=jnp.float32)
                    e = jnp.exp(s).astype(jnp.bfloat16)
                    prob[t, i, pl.ds(j * ROWS, ROWS)] = jnp.minimum(e, m)

        each(6, weigh)

        def gather_values(i):
            total(p, V + i).wait_recv()

            def one(t):
                paired, low, high, split = unit_of(t)
                lhs = [[], [], [], []]
                for j in range(SPAN):
                    is_low = j < split
                    block = jnp.where(is_low, low - j, high - j + split)
                    v = vr[p, i, block]
                    ones = jnp.ones((16, ROWS), jnp.bfloat16)
                    lhs[0].append(jnp.where(is_low, v, 0))
                    lhs[1].append(jnp.where(is_low, ones, 0))
                    lhs[2].append(jnp.where(is_low, 0, v))
                    lhs[3].append(jnp.where(is_low, 0, ones))
                lhs = jnp.concatenate([jnp.concatenate(part, axis=1) for part in lhs], axis=0)
                n = dot(lhs, prob[t, i])

                def finish(side, qb):
                    base = side * (HEAD + 16)
                    out = n[base:base + HEAD] / n[base + HEAD:base + HEAD + 1]
                    stage_a[i, qb] = out.astype(jnp.bfloat16)

                    @pl.when(qb != me)
                    def _():
                        back_copy(p, i, qb).start()

                finish(0, low)

                @pl.when(paired)
                def _():
                    finish(1, high)

            each(6, one)
            ar[p, i, me] = stage_a[i, me]

        gather_values(0)
        gather_values(1)

        @pl.when(first)
        def _():
            wide_out_total().wait()

        def project_out(i):
            total(p, A + i).wait_recv()
            part = ar[p, i].reshape(512, ROWS).T
            for t in range(4):
                cols = pl.ds(t * 256, 256)
                before = xs[:, cols].astype(jnp.float32) if i == 0 else mixed[:, cols]
                mixed[:, cols] = before + dot(part, wa[3, pl.ds(i * 512, 512), cols])

        project_out(0)
        project_out(1)
        nb[...] = rms(mixed[...], gain_ref[1:2]).astype(jnp.bfloat16)

        @pl.when(first)
        def _():
            wide(0).wait()

        def expand(t):
            cols = pl.ds(pl.multiple_of(t * 1024, 1024), 1024)
            hidden[:, cols] = gelu(dot(nb[...], wu[:, cols])).astype(jnp.bfloat16)

        each(FF // 1024, expand)

        for kind in (K, Q, V, V + 1, A, A + 1):
            total(p, kind).wait_send()

        @pl.when(first)
        def _():
            wide(1).wait()

        def lower(t):
            @pl.when(t < 4)
            def _():
                cols = pl.ds(pl.multiple_of(t * 256, 256), 256)
                o_ref[:, cols] = (mixed[:, cols] + dot(hidden[...], wd[:, cols])).astype(
                    jnp.bfloat16
                )

            n = lax.div(t, 2)
            odd = t - 2 * n

            @pl.when(first & (odd == 1))
            def _():
                swap_out(n)

            @pl.when(first & (odd == 0) & (t > 0))
            def _():
                compose(n - 1)

        each(5, lower)

        @pl.when(first)
        def _():
            each(2, scan)
            each(2, hand_over)
            each(2, collect)

            @pl.when((h + y + core) == 0)
            def _():
                xs[...] = x_ref[...]

        return carry

    theirs = pl.ds(pl.multiple_of((1 - core) * 128, 128), 128)
    mine = pl.ds(pl.multiple_of(core * 128, 128), 128)
    is_low = core == 0

    def half(n):
        return pl.ds(pl.multiple_of(n * 512, 512), 512)

    def low_gain(n):
        return jnp.where(is_low, coarse_ref[:, half(n)], gains[8, :, half(n)])

    def high_gain(n):
        return jnp.where(is_low, gains[8, :, half(n)], coarse_ref[:, half(n)])

    def swap_copy(n):
        return remote(
            fine.at[n, theirs], half_in.at[n], csend_sem.at[0, n], crecv_sem.at[0, n], partner
        )

    def give_copy(n):
        return remote(
            given.at[n], corrected.at[n], csend_sem.at[1, n], crecv_sem.at[1, n], partner
        )

    def depth_copy(n, trip, i):
        step = depth_step(i)
        dev, dest = depth_peer(*step)
        if trip == 0:
            src = comp.at[n, pl.ds(pl.multiple_of(dest * 16, 16), 16)]
            dst = depth_a.at[n, chip]
        else:
            src, dst = depth_u.at[n, dest], depth_r.at[n, chip]
        return remote(src, dst, dsend_sem.at[n, trip], drecv_sem.at[n, trip], dev)

    def depth_total(n, trip):
        some = (depth_a, depth_r)[trip].at[n, pl.ds(0, 7)]
        return remote(some, some, dsend_sem.at[n, trip], drecv_sem.at[n, trip], partner)

    def swap_out(n):
        lead = jnp.where((h + y + core) == 0, 0.0, 1.0)
        a = o_ref[:, half(n)].astype(jnp.float32)
        b = (lead * coarse_ref[:, half(n)]) * x_ref[:, half(n)].astype(jnp.float32)
        fine[n] = (a - b).astype(jnp.bfloat16)
        swap_copy(n).start()

    def compose(n):
        @pl.when(n == 0)
        def _():
            gain_total().wait()

        swap_copy(n).wait()
        own, other = fine[n, mine, :].astype(jnp.float32), half_in[n].astype(jnp.float32)
        low, high = jnp.where(is_low, own, other), jnp.where(is_low, other, own)
        comp[n] = (high + high_gain(n) * low).astype(jnp.bfloat16)
        each(7, lambda i: depth_copy(n, 0, i).start())
        depth_a[n, chip] = comp[n, pl.ds(pl.multiple_of(chip * 16, 16), 16), :]

    def scan(n):
        depth_total(n, 0).wait_recv()
        u = jnp.zeros((16, 512), jnp.float32)
        for k in range(8):
            depth_u[n, k] = u.astype(jnp.bfloat16)
            u = depth_a[n, k].astype(jnp.float32) + gains[k, :, half(n)] * u
        each(7, lambda i: depth_copy(n, 1, i).start())
        depth_r[n, chip] = depth_u[n, chip]

    def hand_over(n):
        depth_total(n, 1).wait_recv()
        back = jnp.concatenate([depth_r[n, k] for k in range(8)], axis=0).astype(jnp.float32)
        own, other = fine[n, mine, :].astype(jnp.float32), half_in[n].astype(jnp.float32)
        after = jnp.where(is_low, own, other) + low_gain(n) * back
        given[n] = jnp.where(is_low, after, back).astype(jnp.bfloat16)
        give_copy(n).start()
        xs[mine, half(n)] = jnp.where(is_low, back, after).astype(jnp.bfloat16)

    def collect(n):
        depth_total(n, 0).wait_send()
        depth_total(n, 1).wait_send()
        give_copy(n).wait()
        xs[theirs, half(n)] = corrected[n]

    lax.fori_loop(0, 2, one_pass, 0)


def on_device(interfaces, doc_ids, w_attn, w_up, w_down, norm_gains, coarse_gain):
    x = interfaces.reshape(ROWS, D)
    doc = doc_ids.reshape(GROUPS, 1, ROWS)
    bf, f32 = jnp.bfloat16, jnp.float32
    vmem = pl.BlockSpec(memory_space=pltpu.VMEM)
    hbm = pl.BlockSpec(memory_space=pl.ANY)
    out = pl.pallas_call(
        kernel,
        out_shape=pltpu.VMEM((ROWS, D), bf),
        in_specs=[hbm] * 7,
        out_specs=vmem,
        scratch_shapes=[
            pltpu.VMEM((ROWS, D), bf),
            pltpu.VMEM((GROUPS, 1, ROWS), jnp.int32),
            pltpu.VMEM((2, D), f32),
            pltpu.VMEM((1, D), f32),
            pltpu.VMEM((4, D, D), bf),
            pltpu.VMEM((D, FF), bf),
            pltpu.VMEM((FF, D), bf),
            pltpu.VMEM((ROWS, D), bf),
            pltpu.VMEM((ROWS, D), bf),
            pltpu.VMEM((2, GROUPS, ROWS, LANES), bf),
            pltpu.VMEM((2, GROUPS, HEAD, ROWS), bf),
            pltpu.VMEM((2, GROUPS, ROWS, LANES), bf),
            pltpu.VMEM((2, GROUPS, ROWS, LANES), bf),
            pltpu.VMEM((2, 2, GROUPS, HEAD, ROWS), bf),
            pltpu.VMEM((GROUPS * SPAN, ROWS, ROWS), bf),
            pltpu.VMEM((6, 2, SPAN * ROWS, ROWS), bf),
            pltpu.VMEM((2, GROUPS, HEAD, ROWS), bf),
            pltpu.VMEM((2, 2, GROUPS, HEAD, ROWS), bf),
            pltpu.VMEM((ROWS, D), f32),
            pltpu.VMEM((ROWS, FF), bf),
            pltpu.VMEM((10, 1, D), f32),
            pltpu.VMEM((2, ROWS, 512), bf),
            pltpu.VMEM((2, 128, 512), bf),
            pltpu.VMEM((2, 128, 512), bf),
            pltpu.VMEM((2, 8, 16, 512), bf),
            pltpu.VMEM((2, 8, 16, 512), bf),
            pltpu.VMEM((2, 8, 16, 512), bf),
            pltpu.VMEM((2, 128, 512), bf),
            pltpu.VMEM((2, 128, 512), bf),
            pltpu.SemaphoreType.DMA((5,)),
            pltpu.SemaphoreType.DMA((3, 4)),
            pltpu.SemaphoreType.DMA((3,)),
            pltpu.SemaphoreType.DMA((6,)),
            pltpu.SemaphoreType.DMA((2, 6)),
            pltpu.SemaphoreType.DMA((2,)),
            pltpu.SemaphoreType.DMA((2, 2)),
            pltpu.SemaphoreType.DMA((2, 2)),
            pltpu.SemaphoreType.DMA((3, 2)),
            pltpu.SemaphoreType.DMA((3, 2)),
        ],
        compiler_params=pltpu.CompilerParams(
            collective_id=0, has_side_effects=True, vmem_limit_bytes=60 * 2**20
        ),
        name="cycle",
    )(
        x,
        doc,
        norm_gains.reshape(2, D),
        coarse_gain.reshape(1, D),
        w_attn.reshape(4, D, D),
        w_up.reshape(D, FF),
        w_down.reshape(FF, D),
    )
    return out.reshape(1, 1, ROWS, D)


def solution(mesh):
    split = Mesh(
        mesh.devices.reshape(2, 4, 2, 4, 2), ("depth_0", "depth_1", "depth_2", "seq_0", "seq_1")
    )
    in_specs = (
        P(DEPTH, None, SEQ, None),
        P(),
        P(DEPTH, None, None, None, None),
        P(DEPTH, None, None, None),
        P(DEPTH, None, None, None),
        P(DEPTH, None, None, None),
        P(DEPTH, None),
    )
    out_specs = P(DEPTH, None, SEQ, None)
    return jax.shard_map(
        on_device, mesh=split, in_specs=in_specs, out_specs=out_specs, check_vma=False
    )
```

time: 374 us -> 91.1 us (0.24); the launches traced: 369 us -> 90.7 us
  waiting for transfers between devices: 197 us -> 0 us
  matrix products: 124 us -> 0 us
  Pallas kernels: 0 us -> 89.9 us
  blocking collectives: 16.5 us -> 0 us
  between operations: 13.9 us -> 0.01 us
  other arithmetic: 13 us -> 0 us
    all_gather x7 -> x0, waiting for transfers between devices: 197 us -> none  [the longest x4 144 us: whole_of(): x = lax.all_gather(x, axis, axis=dim, tiled=True)]
    dot_general x14 -> x0, matrix products: 124 us -> none  [the longest x2 30.5 us: one_layer(): jnp.einsum('shqk,skhd->shqd', weights.astype(jnp.bfloat16), value_heads,...]
    pallas_call x0 -> x1, Pallas kernels: none -> 89.9 us  [on_device(): pl.pallas_call(kernel, out_shape=pltpu.VMEM((ROWS, D), bf), in_specs=[hbm...]
    all_gather x3 -> x0, blocking collectives: 16.5 us -> none  [carried_in(): lax.all_gather(part.astype(kind), axis)]
    convert_element_type x9 -> x0, other arithmetic: 8.17 us -> none  [the longest x4 5.11 us: carried_in(): part.astype(kind)]
    reduce_sum x2 -> x0, other arithmetic: 4.19 us -> none  [rms_norm(): jnp.mean(value_tensor * value_tensor, axis=-1, keepdims=True) + 1e-05]
  transfers between devices with their start and end apart: 8 -> 0, of which waited for: 7 -> 0; matrix products, arithmetic and copies ran while one was open for 15% -> 0% of each run, Pallas kernels for 0% -> 0%
where the time goes in v2:
time: 91.1 us; the launch traced here: 90.7 us
  Pallas kernels  89.9 us (99%)
    pallas_call x1, Pallas kernels, on_device(): pl.pallas_call(kernel, out_shape=pltpu.VMEM((ROWS, D), bf), in_specs=[hbm...  89.9 us

profile of v2, /device:TPU:1, one launch (start us, length us, event | category | flops | bytes accessed | tf_op | source)
XLA Modules:
  0.0 90.7 jit_solution(6731798680629973121)
XLA Ops:
  0.0 89.9 %cycle.1 = bf16[256,1024]{1,0:T(8,128)(2,1)S(1)} custom-call(bf16[256,1024]{1,0:T(8,128)(2,1)} %bitcast.11, s32[8,1,256]{2,1,0:T(1,128)} %bitcast.12, f32[2,1024]{1,0:T(2,128)} %bitcast.13, f32[1,1024]{1,0:T(1,128)} %coarse_hbm.1, bf16[4,1024,1024]{2,1,0:T(8,128)(2,1)} %bitcast.8, bf16[1024,4096]{1,0:T(8,128)(2,1)} %bitcast.9, bf16[4096,1024]{1,0:T(8,128)(2,1)} %bitcast.10), custom_call_target="tpu_custom_call" | custom-call | tf_op jit(solution)/shard_map/cycle/pallas_call | solution.py:480
  89.9 0.8 copy.9

commit v3 on v2

--- a/solution.py
+++ b/solution.py
@@ -62,7 +62,7 @@
     x_hbm, doc_hbm, gain_hbm, coarse_hbm, wa_hbm, wu_hbm, wd_hbm, o_ref,
     x_ref, doc_ref, gain_ref, coarse_ref, wa, wu, wd, xs, nb, stage, stage_v, kr, qr, vr, mask, prob, stage_a, ar, mixed, hidden,
     gains, fine, half_in, comp, depth_a, depth_u, depth_r, given, corrected,
-    in_sem, w_sem, wide_sem, send_sem, recv_sem, g_sem, dsend_sem, drecv_sem, csend_sem, crecv_sem,
+    in_sem, w_sem, wide_sem, send_sem, recv_sem, q_sem, g_sem, dsend_sem, drecv_sem, csend_sem, crecv_sem,
 ):
     h, y, core = (lax.axis_index(a) for a in DEPTH)
     z, c = (lax.axis_index(a) for a in SEQ)
@@ -147,7 +147,12 @@
             src, dst = stage.at[1, dest], qr.at[p, me]
         else:
             src, dst = stage_v.at[kind - V, dest], vr.at[p, kind - V, me]
-        return remote(src, dst, send_sem.at[kind], recv_sem.at[p, kind], dev)
+        got = q_sem.at[p, me] if kind == Q else recv_sem.at[p, kind]
+        return remote(src, dst, send_sem.at[kind], got, dev)
+
+    def query_arrival(p, who):
+        dst = qr.at[p, who]
+        return remote(dst, dst, send_sem.at[Q], q_sem.at[p, who], partner)
 
     def back_copy(p, i, dest):
         pz = lax.div(dest, 2)
@@ -196,9 +201,6 @@
                         seq_copy(p, kind, 2 * u + 1).start()
 
             each(4, tile)
-            if kind == V:
-                each(7, lambda i: seq_copy(p, V, i).start())
-                each(7, lambda i: seq_copy(p, V + 1, i).start())
 
         def store_k(base, r):
             stage[0, base] = r[:, :LANES]
@@ -220,6 +222,8 @@
         project(0, Q, store_q)
         qr[p, me] = stage[1, me]
         project(2, V, store_v)
+        each(7, lambda i: seq_copy(p, V, i).start())
+        each(7, lambda i: seq_copy(p, V + 1, i).start())
         for i in range(2):
             vr[p, i, me] = stage_v[i, me]
 
@@ -254,11 +258,19 @@
             lax.fori_loop(0, GROUPS, build, 0)
 
         total(p, K).wait_recv()
-        total(p, Q).wait_recv()
         own = jnp.where(me >= 4, me - 4, jnp.where((me == 0) | (me == 3), 4, 5))
 
         def unit_of(t):
-            unit = lax.rem(own + 1 + t, 6)
+            g = lax.div(t, 2)
+            near = jnp.where((z == 1) | (z == 2), 0, 2)
+            full = jnp.where(lax.rem(g + z, 2) == lax.rem(z, 2), near, 2 - near)
+            late = jnp.where(g == 1, near, 2 - near)
+            base = jnp.where(
+                z < 2,
+                jnp.where(g == 0, 4, late),
+                jnp.where(g == 2, 4, full),
+            )
+            unit = base + lax.rem(own + t, 2)
             paired = unit >= 4
             low = jnp.where(paired, unit - 4, unit + 4)
             high = jnp.where(paired, 3 - low, low)
@@ -266,7 +278,16 @@
             return paired, low, high, split
 
         def weigh(t):
-            _, low, high, split = unit_of(t)
+            paired, low, high, split = unit_of(t)
+
+            @pl.when(low != me)
+            def _():
+                query_arrival(p, low).wait_recv()
+
+            @pl.when(paired & (high != me))
+            def _():
+                query_arrival(p, high).wait_recv()
+
             for j in range(SPAN):
                 is_low = j < split
                 qb = jnp.where(is_low, low, high)
@@ -286,8 +307,8 @@
         def gather_values(i):
             total(p, V + i).wait_recv()
 
-            def one(t):
-                paired, low, high, split = unit_of(t)
+            def combine(t):
+                _, low, high, split = unit_of(t)
                 lhs = [[], [], [], []]
                 for j in range(SPAN):
                     is_low = j < split
@@ -299,24 +320,29 @@
                     lhs[2].append(jnp.where(is_low, 0, v))
                     lhs[3].append(jnp.where(is_low, 0, ones))
                 lhs = jnp.concatenate([jnp.concatenate(part, axis=1) for part in lhs], axis=0)
-                n = dot(lhs, prob[t, i])
-
-                def finish(side, qb):
-                    base = side * (HEAD + 16)
-                    out = n[base:base + HEAD] / n[base + HEAD:base + HEAD + 1]
-                    stage_a[i, qb] = out.astype(jnp.bfloat16)
-
-                    @pl.when(qb != me)
+                return dot(lhs, prob[t, i])
+
+            def finish(n, side, qb):
+                base = side * (HEAD + 16)
+                out = n[base:base + HEAD] / n[base + HEAD:base + HEAD + 1]
+                stage_a[i, qb] = out.astype(jnp.bfloat16)
+
+                @pl.when(qb != me)
+                def _():
+                    back_copy(p, i, qb).start()
+
+            def two(s):
+                units = (5 - 2 * s, 4 - 2 * s)
+                sums = [combine(t) for t in units]
+                for t, n in zip(units, sums):
+                    paired, low, high, _ = unit_of(t)
+                    finish(n, 0, low)
+
+                    @pl.when(paired)
                     def _():
-                        back_copy(p, i, qb).start()
-
-                finish(0, low)
-
-                @pl.when(paired)
-                def _():
-                    finish(1, high)
-
-            each(6, one)
+                        finish(n, 1, high)
+
+            each(3, two)
             ar[p, i, me] = stage_a[i, me]
 
         gather_values(0)
@@ -343,10 +369,10 @@
             wide(0).wait()
 
         def expand(t):
-            cols = pl.ds(pl.multiple_of(t * 1024, 1024), 1024)
+            cols = pl.ds(pl.multiple_of(t * 2048, 2048), 2048)
             hidden[:, cols] = gelu(dot(nb[...], wu[:, cols])).astype(jnp.bfloat16)
 
-        each(FF // 1024, expand)
+        each(FF // 2048, expand)
 
         for kind in (K, Q, V, V + 1, A, A + 1):
             total(p, kind).wait_send()
@@ -363,24 +389,27 @@
                     jnp.bfloat16
                 )
 
-            n = lax.div(t, 2)
-            odd = t - 2 * n
-
-            @pl.when(first & (odd == 1))
+            @pl.when(t < 4)
             def _():
-                swap_out(n)
-
-            @pl.when(first & (odd == 0) & (t > 0))
+                swap_out(t)
+
+            @pl.when(t > 0)
             def _():
-                compose(n - 1)
-
-        each(5, lower)
+                compose(t - 1)
 
         @pl.when(first)
         def _():
-            each(2, scan)
-            each(2, hand_over)
-            each(2, collect)
+            each(5, lower)
+
+        @pl.when(p == 1)
+        def _():
+            o_ref[...] = (mixed[...] + dot(hidden[...], wd[...])).astype(jnp.bfloat16)
+
+        @pl.when(first)
+        def _():
+            each(4, scan)
+            each(4, hand_over)
+            each(4, collect)
 
             @pl.when((h + y + core) == 0)
             def _():
@@ -393,7 +422,7 @@
     is_low = core == 0
 
     def half(n):
-        return pl.ds(pl.multiple_of(n * 512, 512), 512)
+        return pl.ds(pl.multiple_of(n * 256, 256), 256)
 
     def low_gain(n):
         return jnp.where(is_low, coarse_ref[:, half(n)], gains[8, :, half(n)])
@@ -446,7 +475,7 @@
 
     def scan(n):
         depth_total(n, 0).wait_recv()
-        u = jnp.zeros((16, 512), jnp.float32)
+        u = jnp.zeros((16, 256), jnp.float32)
         for k in range(8):
             depth_u[n, k] = u.astype(jnp.bfloat16)
             u = depth_a[n, k].astype(jnp.float32) + gains[k, :, half(n)] * u
@@ -504,24 +533,25 @@
             pltpu.VMEM((ROWS, D), f32),
             pltpu.VMEM((ROWS, FF), bf),
             pltpu.VMEM((10, 1, D), f32),
-            pltpu.VMEM((2, ROWS, 512), bf),
-            pltpu.VMEM((2, 128, 512), bf),
-            pltpu.VMEM((2, 128, 512), bf),
-            pltpu.VMEM((2, 8, 16, 512), bf),
-            pltpu.VMEM((2, 8, 16, 512), bf),
-            pltpu.VMEM((2, 8, 16, 512), bf),
-            pltpu.VMEM((2, 128, 512), bf),
-            pltpu.VMEM((2, 128, 512), bf),
+            pltpu.VMEM((4, ROWS, 256), bf),
+            pltpu.VMEM((4, 128, 256), bf),
+            pltpu.VMEM((4, 128, 256), bf),
+            pltpu.VMEM((4, 8, 16, 256), bf),
+            pltpu.VMEM((4, 8, 16, 256), bf),
+            pltpu.VMEM((4, 8, 16, 256), bf),
+            pltpu.VMEM((4, 128, 256), bf),
+            pltpu.VMEM((4, 128, 256), bf),
             pltpu.SemaphoreType.DMA((5,)),
             pltpu.SemaphoreType.DMA((3, 4)),
             pltpu.SemaphoreType.DMA((3,)),
             pltpu.SemaphoreType.DMA((6,)),
             pltpu.SemaphoreType.DMA((2, 6)),
+            pltpu.SemaphoreType.DMA((2, 8)),
             pltpu.SemaphoreType.DMA((2,)),
-            pltpu.SemaphoreType.DMA((2, 2)),
-            pltpu.SemaphoreType.DMA((2, 2)),
-            pltpu.SemaphoreType.DMA((3, 2)),
-            pltpu.SemaphoreType.DMA((3, 2)),
+            pltpu.SemaphoreType.DMA((4, 2)),
+            pltpu.SemaphoreType.DMA((4, 2)),
+            pltpu.SemaphoreType.DMA((3, 4)),
+            pltpu.SemaphoreType.DMA((3, 4)),
         ],
         compiler_params=pltpu.CompilerParams(
             collective_id=0, has_side_effects=True, vmem_limit_bytes=60 * 2**20

time: 91.1 us -> 87.6 us (0.962)
  Pallas kernels: 89.9 us -> 86.6 us
    pallas_call x1, Pallas kernels: 89.9 us -> 86.6 us  [on_device(): pl.pallas_call(kernel, out_shape=pltpu.VMEM((ROWS, D), bf), in_specs=[hbm...]
where the time goes in v3:
time: 87.6 us; the launch traced here: 87.4 us
  Pallas kernels  86.6 us (99%)
    pallas_call x1, Pallas kernels, on_device(): pl.pallas_call(kernel, out_shape=pltpu.VMEM((ROWS, D), bf), in_specs=[hbm...  86.6 us

profile of v3, /device:TPU:1, one launch (start us, length us, event | category | flops | bytes accessed | tf_op | source)
XLA Modules:
  0.0 87.4 jit_solution(18256688760103291544)
XLA Ops:
  0.0 86.6 %cycle.1 = bf16[256,1024]{1,0:T(8,128)(2,1)S(1)} custom-call(bf16[256,1024]{1,0:T(8,128)(2,1)} %bitcast.11, s32[8,1,256]{2,1,0:T(1,128)} %bitcast.12, f32[2,1024]{1,0:T(2,128)} %bitcast.13, f32[1,1024]{1,0:T(1,128)} %coarse_hbm.1, bf16[4,1024,1024]{2,1,0:T(8,128)(2,1)} %bitcast.8, bf16[1024,4096]{1,0:T(8,128)(2,1)} %bitcast.9, bf16[4096,1024]{1,0:T(8,128)(2,1)} %bitcast.10), custom_call_target="tpu_custom_call" | custom-call | tf_op jit(solution)/shard_map/cycle/pallas_call | solution.py:509
  86.6 0.8 copy.9

commit v4 on v3

--- a/solution.py
+++ b/solution.py
@@ -44,8 +44,8 @@
 
 
 def depth_step(i):
-    u = lax.div(i + 1, 4)
-    return u, i + 1 - 4 * u
+    u = lax.div(i, 4)
+    return 1 - u, row_step(i - 4 * u)
 
 
 def gelu(x):

time: 87.6 us -> 87 us (level)
  no operation moved by 1% of the time
where the time goes in v4:
time: 87 us; the launch traced here: 86.9 us
  Pallas kernels  86.1 us (99%)
    pallas_call x1, Pallas kernels, on_device(): pl.pallas_call(kernel, out_shape=pltpu.VMEM((ROWS, D), bf), in_specs=[hbm...  86.1 us

profile of v4, /device:TPU:1, one launch (start us, length us, event | category | flops | bytes accessed | tf_op | source)
XLA Modules:
  0.0 86.9 jit_solution(2994692002594671797)
XLA Ops:
  0.0 86.1 %cycle.1 = bf16[256,1024]{1,0:T(8,128)(2,1)S(1)} custom-call(bf16[256,1024]{1,0:T(8,128)(2,1)} %bitcast.11, s32[8,1,256]{2,1,0:T(1,128)} %bitcast.12, f32[2,1024]{1,0:T(2,128)} %bitcast.13, f32[1,1024]{1,0:T(1,128)} %coarse_hbm.1, bf16[4,1024,1024]{2,1,0:T(8,128)(2,1)} %bitcast.8, bf16[1024,4096]{1,0:T(8,128)(2,1)} %bitcast.9, bf16[4096,1024]{1,0:T(8,128)(2,1)} %bitcast.10), custom_call_target="tpu_custom_call" | custom-call | tf_op jit(solution)/shard_map/cycle/pallas_call | solution.py:509
  86.1 0.8 copy.9

commit v5 on v4

--- a/solution.py
+++ b/solution.py
@@ -368,11 +368,7 @@
         def _():
             wide(0).wait()
 
-        def expand(t):
-            cols = pl.ds(pl.multiple_of(t * 2048, 2048), 2048)
-            hidden[:, cols] = gelu(dot(nb[...], wu[:, cols])).astype(jnp.bfloat16)
-
-        each(FF // 2048, expand)
+        hidden[...] = gelu(dot(nb[...], wu[...])).astype(jnp.bfloat16)
 
         for kind in (K, Q, V, V + 1, A, A + 1):
             total(p, kind).wait_send()

time: 87 us -> 86.7 us (level)
  no operation moved by 1% of the time
where the time goes in v5:
time: 86.7 us; the launch traced here: 86.5 us
  Pallas kernels  85.7 us (99%)
    pallas_call x1, Pallas kernels, on_device(): pl.pallas_call(kernel, out_shape=pltpu.VMEM((ROWS, D), bf), in_specs=[hbm...  85.7 us

profile of v5, /device:TPU:1, one launch (start us, length us, event | category | flops | bytes accessed | tf_op | source)
XLA Modules:
  0.0 86.5 jit_solution(682368933192193206)
XLA Ops:
  0.0 85.7 %cycle.1 = bf16[256,1024]{1,0:T(8,128)(2,1)S(1)} custom-call(bf16[256,1024]{1,0:T(8,128)(2,1)} %bitcast.11, s32[8,1,256]{2,1,0:T(1,128)} %bitcast.12, f32[2,1024]{1,0:T(2,128)} %bitcast.13, f32[1,1024]{1,0:T(1,128)} %coarse_hbm.1, bf16[4,1024,1024]{2,1,0:T(8,128)(2,1)} %bitcast.8, bf16[1024,4096]{1,0:T(8,128)(2,1)} %bitcast.9, bf16[4096,1024]{1,0:T(8,128)(2,1)} %bitcast.10), custom_call_target="tpu_custom_call" | custom-call | tf_op jit(solution)/shard_map/cycle/pallas_call | solution.py:505
  85.7 0.8 copy.9
